TPU v7x, 256 devices: a whole 4x4x8 slice. The times are simulated.
256 devices in a mesh: row: 32 (over y, z), col: 8 (over x, core).
Axes of the slice: x: 4, y: 4, z: 8, core: 2. Of those that a mesh axis runs over, the one named last changes fastest.
Arguments:
- embedding: bfloat16 [8, 32, 48, 256], P('col', 'row'), may hold values from -0.3984375 to 0.3984375
- preference: float32 [12288], P('row'), may hold values from -2.5 to -0.5
Outputs:
- responsibility: float32 [12288, 12288], P('row', 'col')
- availability: float32 [12288, 12288], P('row', 'col')
All inputs are finite; a program needn't handle non-finite values.
Results may differ from a plain program's by a relative error of at most 0.0003.
Values may be sent and summed in bfloat16 or wider, within the bound.
A program may use at most 64 MiB of HBM per device.

v0:
```python
import jax
import jax.numpy as jnp
from jax import lax
from jax.sharding import PartitionSpec as P

ITERS = 2
DAMPING = 0.5


def broadcast(block, axis, source):
    block = jnp.where(lax.axis_index(axis) == source, block, jnp.zeros_like(block))
    return lax.psum(block, axis)


def similarity(row_emb, col_emb, row_start, col_start, pref_rows):
    cross = lax.dot_general(
        row_emb, col_emb, (((1,), (1,)), ((), ())), preferred_element_type=jnp.float32
    )
    row_vals = row_emb.astype(jnp.float32)
    col_vals = col_emb.astype(jnp.float32)
    row_sq = jnp.sum(row_vals * row_vals, axis=1)
    col_sq = jnp.sum(col_vals * col_vals, axis=1)
    dist = 2.0 * cross - row_sq[:, None] - col_sq[None, :]
    row_ids = row_start + jnp.arange(row_emb.shape[0], dtype=jnp.int32)
    col_ids = col_start + jnp.arange(col_emb.shape[0], dtype=jnp.int32)
    diagonal = row_ids[:, None] == col_ids[None, :]
    return (jnp.where(diagonal, pref_rows[:, None], dist), diagonal)


def top_two(summed):
    first = jnp.max(summed, axis=1)
    hits = summed == first[:, None]
    repeats = jnp.sum(hits.astype(jnp.int32), axis=1)
    others = jnp.max(jnp.where(hits, -jnp.inf, summed), axis=1)
    second = jnp.where(repeats > 1, first, others)
    return (first, second)


def local(embedding, preference):
    rows_n = lax.axis_size("row")
    cols_n = lax.axis_size("col")
    row_idx = lax.axis_index("row")
    col_idx = lax.axis_index("col")
    mol = embedding.shape[2]
    width = embedding.shape[3]
    row_count = mol * cols_n
    col_count = mol * rows_n
    column_block = lax.all_gather(embedding, "row", axis=1, tiled=True).reshape(col_count, width)
    offset = row_idx * cols_n % rows_n
    root = row_idx * cols_n // rows_n
    own_slice = lax.dynamic_slice_in_dim(column_block, offset * mol, row_count, 0)
    row_block = broadcast(own_slice, "col", root)
    row_start = row_idx * row_count
    col_start = col_idx * col_count
    sim, diagonal = similarity(row_block, column_block, row_start, col_start, preference)
    resp = jnp.zeros_like(sim)
    avail = jnp.zeros_like(sim)
    for step in range(ITERS):
        summed = avail + sim
        local_first, local_second = top_two(summed)
        firsts, seconds = (
            lax.all_gather(local_first, "col", axis=0, tiled=True),
            lax.all_gather(local_second, "col", axis=0, tiled=True),
        )
        firsts = firsts.reshape(cols_n, row_count)
        seconds = seconds.reshape(cols_n, row_count)
        first = jnp.max(firsts, axis=0)
        at_top = firsts == first[None, :]
        repeats = jnp.sum(at_top.astype(jnp.int32), axis=0)
        others = jnp.max(jnp.where(at_top, -jnp.inf, firsts), axis=0)
        second = jnp.where(repeats > 1, first, jnp.maximum(jnp.max(seconds, axis=0), others))
        fresh = sim - jnp.where(summed == first[:, None], second[:, None], first[:, None])
        resp = DAMPING * resp + (1.0 - DAMPING) * fresh
        positive = jnp.where(diagonal, resp, jnp.maximum(resp, 0.0))
        colsum = lax.psum(jnp.sum(positive, axis=0), "row")
        renew = colsum[None, :] - positive
        renew = jnp.where(diagonal, renew, jnp.minimum(renew, 0.0))
        avail = DAMPING * avail + (1.0 - DAMPING) * renew
    return (resp, avail)


def solution(mesh):
    placed = (P("col", "row", None, None), P("row"))
    return jax.shard_map(
        local,
        mesh=mesh,
        in_specs=placed,
        out_specs=(P("row", "col"), P("row", "col")),
        check_vma=False,
    )
```

profile of v0, /device:TPU:32, one launch (start us, length us, event | category | flops | bytes accessed | tf_op | source)
XLA Modules:
  0.0 337.2 jit_solution(9302854536227118023)
XLA Ops:
  7.2 0.0 all-reduce.2.cloned.1.call-start
  7.2 52.2 %all_gather.15 = bf16[1,32,48,256]{3,2,0,1:T(8,128)(2,1)S(1)} all-gather(bf16[1,1,48,256]{3,2,0,1:T(8,128)(2,1)} %bitcast.12), channel_id=1, replica_groups=mesh['row'=32,'col'=8] {'row'}, dimensions={1}, use_global_device_ids=true | all-gather | bytes 811008 | tf_op jit(solution)/shard_map/all_gather | solution.py:48
  59.5 0.7 dynamic-slice_select_fusion
  60.2 0.0 all-reduce.2.cloned.1.call-update
  60.2 0.3 multiply_reduce_fusion
  60.5 0.1 sub.47
  60.6 62.6 %all-reduce.2.cloned.1.call-done = bf16[384,256]{1,0:T(8,128)(2,1)} async-done(((bf16[384,256]{1,0:T(8,128)(2,1)}), bf16[384,256]{1,0:T(8,128)(2,1)}) %all-reduce.2.cloned.1.call-update) | async-done | bytes 196624 | tf_op jit(solution)/shard_map/psum | solution.py:12
  123.2 1.1 multiply_reduce_fusion.1
  124.3 1.7 fusion.15
  126.0 0.4 fusion.3
  126.4 0.4 fusion.2
  126.8 11.2 %all-gather = f32[8,1,384]{2,1,0:T(1,128)S(1)} all-gather(f32[1,1,384]{2,1,0:T(1,128)S(1)} %reshape.67), channel_id=1, replica_groups=mesh['row'=32,'col'=8] {'col'}, dimensions={0}, use_global_device_ids=true | all-gather | bytes 13824 | tf_op jit(solution)/shard_map/all_gather | solution.py:62
  138.1 11.2 %all-gather.1 = f32[8,1,384]{2,1,0:T(1,128)S(1)} all-gather(f32[1,1,384]{2,1,0:T(1,128)S(1)} %reshape.69), channel_id=1, replica_groups=mesh['row'=32,'col'=8] {'col'}, dimensions={0}, use_global_device_ids=true | all-gather | bytes 13824 | tf_op jit(solution)/shard_map/all_gather | solution.py:63
  149.3 0.7 fusion.9
  150.1 72.6 %psum.22 = f32[1536]{0:T(1024)S(1)} all-reduce(f32[1536]{0:T(1024)S(1)} %fusion.9), channel_id=1, replica_groups=mesh['row'=32,'col'=8] {'row'}, use_global_device_ids=true, to_apply=%region_11.12 | all-reduce | flops 1536 | bytes 12288 | tf_op jit(solution)/shard_map/psum | solution.py:75
  222.7 1.3 fusion.14
  224.0 0.4 fusion.4
  224.4 0.4 fusion.5
  224.8 0.6 copy-done
  225.4 11.2 %all-gather.2 = f32[8,1,384]{2,1,0:T(1,128)S(1)} all-gather(f32[1,1,384]{2,1,0:T(1,128)S(1)} %reshape.71), channel_id=1, replica_groups=mesh['row'=32,'col'=8] {'col'}, dimensions={0}, use_global_device_ids=true | all-gather | bytes 13824 | tf_op jit(solution)/shard_map/all_gather | solution.py:62
  236.7 11.2 %all-gather.3 = f32[8,1,384]{2,1,0:T(1,128)S(1)} all-gather(f32[1,1,384]{2,1,0:T(1,128)S(1)} %reshape.73), channel_id=1, replica_groups=mesh['row'=32,'col'=8] {'col'}, dimensions={0}, use_global_device_ids=true | all-gather | bytes 13824 | tf_op jit(solution)/shard_map/all_gather | solution.py:63
  247.9 3.5 %fusion.8 = (f32[1536]{0:T(1024)S(1)}, f32[384,1536]{1,0:T(8,128)}) fusion(s32[1536]{0:T(1024)S(1)} %iota_add_fusion, s32[384]{0:T(512)S(1)} %iota_add_fusion.1, f32[384,1536]{1,0:T(8,128)S(1)} %get-tuple-element.7, f32[384]{0:T(512)S(1)} %maximum_select_fusion, f32[384,1536]{1,0:T(8,128)} %copy-done, f32[384]{0:T(512)S(1)} %reduce_max.96, ...), kind=kLoop, calls=%fused_computation.21 | loop fusion | flops 7666176 | bytes 7097856 | tf_op jit(solution)/shard_map/reduce_sum | solution.py:75
  251.4 74.6 %psum.23 = f32[1536]{0:T(1024)S(1)} all-reduce(f32[1536]{0:T(1024)S(1)} %get-tuple-element.2), channel_id=1, replica_groups=mesh['row'=32,'col'=8] {'row'}, use_global_device_ids=true, to_apply=%region_20.21 | all-reduce | flops 1536 | bytes 12288 | tf_op jit(solution)/shard_map/psum | solution.py:75
  326.0 4.3 %fusion.7 = f32[384,1536]{1,0:T(8,128)} fusion(f32[384,1536]{1,0:T(8,128)} %get-tuple-element.3, f32[384,1536]{1,0:T(8,128)S(1)} %get-tuple-element.7, f32[1536]{0:T(1024)S(1)} %psum.23, f32[1536]{0:T(1024)S(1)} %psum.22, f32[384]{0:T(512)S(1)} %maximum_select_fusion.1, f32[384]{0:T(512)S(1)} %reduce_max.91, s32[1536]{0:T(1024)S(1)} %iota_add_fusion, ...), kind=kLoop, calls=%fused_computation.17 | loop fusion | flops 10616832 | bytes 7100928 | tf_op jit(solution)/shard_map/add | solution.py:78
  (21 shorter events, 0.3 us)
Async XLA Ops:
  7.2 117.1 %copy-start.1 = (f32[384]{0:T(512)S(1)}, f32[384]{0:T(512)}, u32[]{:S(2)}) copy-start(f32[384]{0:T(512)} %param.3) | copy-start | bytes 4612
  7.2 116.0 %all-reduce.2.cloned.1.call-start = ((), (), s32[]{:S(2)}) async-start(), calls=%async_computation | async-start | bytes 393216 | tf_op jit(solution)/shard_map/psum | solution.py:12
  224.0 1.4 copy-start
Sparse Core Ops, SparseCore 0:
  60.3 62.7 all-reduce.1
where the time goes:
time: 338 us; the launch traced here: 337 us
  blocking collectives  244 us (72%)
  waiting for transfers between devices  62.6 us (19%)
  between operations  14.2 us (4%)
  other arithmetic  13.7 us (4%)
    psum x2, blocking collectives, local(): colsum = lax.psum(jnp.sum(positive, axis=0), 'row')  147 us
    psum x1, waiting for transfers between devices, broadcast(): return lax.psum(block, axis)  62.6 us
    all_gather x1, blocking collectives, local(): lax.all_gather(embedding, 'row', axis=1, tiled=True)  52.2 us
    all_gather x2, blocking collectives, local(): lax.all_gather(local_second, 'col', axis=0, tiled=True)  22.4 us
    all_gather x2, blocking collectives, local(): lax.all_gather(local_first, 'col', axis=0, tiled=True)  22.4 us
  transfers between devices with their start and end apart: 1, of which 1 were waited for; matrix products, arithmetic and copies ran while one was open for 0% of the time, Pallas kernels for 0%

commit v1 on v0

--- a/solution.py
+++ b/solution.py
@@ -2,6 +2,7 @@
 import jax.numpy as jnp
 from jax import lax
 from jax.sharding import PartitionSpec as P
+from jax.lax import all_gather
 
 ITERS = 2
 DAMPING = 0.5
@@ -72,7 +73,8 @@
         fresh = sim - jnp.where(summed == first[:, None], second[:, None], first[:, None])
         resp = DAMPING * resp + (1.0 - DAMPING) * fresh
         positive = jnp.where(diagonal, resp, jnp.maximum(resp, 0.0))
-        colsum = lax.psum(jnp.sum(positive, axis=0), "row")
+        vector = jnp.sum(positive, axis=0)
+        colsum = jnp.sum(all_gather(vector, "row"), 0)
         renew = colsum[None, :] - positive
         renew = jnp.where(diagonal, renew, jnp.minimum(renew, 0.0))
         avail = DAMPING * avail + (1.0 - DAMPING) * renew

time: 338 us -> 284 us (0.84)
  blocking collectives: 244 us -> 190 us
    psum x2 -> x0, blocking collectives: 147 us -> none  [local(): colsum = lax.psum(jnp.sum(positive, axis=0), 'row')]
    all_gather x0 -> x2, blocking collectives: none -> 93.4 us  [local(): colsum = jnp.sum(all_gather(vector, 'row'), 0)]
where the time goes in v1:
time: 284 us
  blocking collectives  190 us (67%)
  waiting for transfers between devices  62.6 us (22%)
  between operations  14.2 us (5%)
  other arithmetic  14 us (5%)
    all_gather x2, blocking collectives, local(): colsum = jnp.sum(all_gather(vector, 'row'), 0)  93.4 us
    psum x1, waiting for transfers between devices, broadcast(): return lax.psum(block, axis)  62.6 us
    all_gather x1, blocking collectives, local(): lax.all_gather(embedding, 'row', axis=1, tiled=True)  52.2 us
    all_gather x2, blocking collectives, local(): lax.all_gather(local_second, 'col', axis=0, tiled=True)  22.4 us
    all_gather x2, blocking collectives, local(): lax.all_gather(local_first, 'col', axis=0, tiled=True)  22.4 us
  transfers between devices with their start and end apart: 1, of which 1 were waited for; matrix products, arithmetic and copies ran while one was open for 0% of the time, Pallas kernels for 0%

profile of v1, /device:TPU:32, one launch (start us, length us, event | category | flops | bytes accessed | tf_op | source)
XLA Modules:
  0.0 283.6 jit_solution(13357901692534469251)
XLA Ops:
  7.2 52.2 %all_gather.27 = bf16[1,32,48,256]{3,2,0,1:T(8,128)(2,1)S(1)} all-gather(bf16[1,1,48,256]{3,2,0,1:T(8,128)(2,1)} %bitcast.12), channel_id=1, replica_groups=mesh['row'=32,'col'=8] {'row'}, dimensions={1}, use_global_device_ids=true | all-gather | bytes 811008 | tf_op jit(solution)/shard_map/all_gather | solution.py:49
  59.5 0.7 dynamic-slice_select_fusion
  60.2 0.3 multiply_reduce_fusion
  60.5 0.1 sub.47
  60.6 62.6 %all-reduce.2.cloned.1.call-done = bf16[384,256]{1,0:T(8,128)(2,1)} async-done(((bf16[384,256]{1,0:T(8,128)(2,1)}), bf16[384,256]{1,0:T(8,128)(2,1)}) %all-reduce.2.cloned.1.call-update) | async-done | bytes 196624 | tf_op jit(solution)/shard_map/psum | solution.py:13
  123.2 1.1 multiply_reduce_fusion.1
  124.3 1.7 fusion.15
  126.0 0.4 fusion.3
  126.4 0.4 fusion.2
  126.8 11.2 %all-gather.2 = f32[8,1,384]{2,1,0:T(1,128)S(1)} all-gather(f32[1,1,384]{2,1,0:T(1,128)S(1)} %reshape.69), channel_id=1, replica_groups=mesh['row'=32,'col'=8] {'col'}, dimensions={0}, use_global_device_ids=true | all-gather | bytes 13824 | tf_op jit(solution)/shard_map/all_gather | solution.py:63
  138.1 11.2 %all-gather.3 = f32[8,1,384]{2,1,0:T(1,128)S(1)} all-gather(f32[1,1,384]{2,1,0:T(1,128)S(1)} %reshape.71), channel_id=1, replica_groups=mesh['row'=32,'col'=8] {'col'}, dimensions={0}, use_global_device_ids=true | all-gather | bytes 13824 | tf_op jit(solution)/shard_map/all_gather | solution.py:64
  149.3 0.7 fusion.9
  150.1 47.6 %all-gather.4 = f32[32,1,1536]{2,1,0:T(1,128)S(1)} all-gather(f32[1,1,1536]{2,1,0:T(1,128)S(1)} %reshape.73), channel_id=2, replica_groups=mesh['row'=32,'col'=8] {'row'}, dimensions={0}, use_global_device_ids=true | all-gather | bytes 202752 | tf_op jit(solution)/shard_map/all_gather | solution.py:77
  197.7 0.1 reduce_sum.95
  197.8 1.3 fusion.14
  199.1 0.4 fusion.4
  199.5 0.4 fusion.5
  199.9 0.6 copy-done
  200.5 11.2 %all-gather.5 = f32[8,1,384]{2,1,0:T(1,128)S(1)} all-gather(f32[1,1,384]{2,1,0:T(1,128)S(1)} %reshape.75), channel_id=1, replica_groups=mesh['row'=32,'col'=8] {'col'}, dimensions={0}, use_global_device_ids=true | all-gather | bytes 13824 | tf_op jit(solution)/shard_map/all_gather | solution.py:63
  211.8 11.2 %all-gather.6 = f32[8,1,384]{2,1,0:T(1,128)S(1)} all-gather(f32[1,1,384]{2,1,0:T(1,128)S(1)} %reshape.77), channel_id=1, replica_groups=mesh['row'=32,'col'=8] {'col'}, dimensions={0}, use_global_device_ids=true | all-gather | bytes 13824 | tf_op jit(solution)/shard_map/all_gather | solution.py:64
  223.0 3.5 %fusion.8 = (f32[1536]{0:T(1024)S(1)}, f32[384,1536]{1,0:T(8,128)}) fusion(s32[1536]{0:T(1024)S(1)} %iota_add_fusion, s32[384]{0:T(512)S(1)} %iota_add_fusion.1, f32[384,1536]{1,0:T(8,128)S(1)} %get-tuple-element.7, f32[384]{0:T(512)S(1)} %maximum_select_fusion, f32[384,1536]{1,0:T(8,128)} %copy-done, f32[384]{0:T(512)S(1)} %reduce_max.96, ...), kind=kLoop, calls=%fused_computation.21 | loop fusion | flops 7666176 | bytes 7097856 | tf_op jit(solution)/shard_map/reduce_sum | solution.py:76
  226.5 45.8 %all-gather.7 = f32[32,1,1536]{2,1,0:T(1,128)S(1)} all-gather(f32[1,1,1536]{2,1,0:T(1,128)S(1)} %reshape.79), channel_id=3, replica_groups=mesh['row'=32,'col'=8] {'row'}, dimensions={0}, use_global_device_ids=true | all-gather | bytes 202752 | tf_op jit(solution)/shard_map/all_gather | solution.py:77
  272.3 0.1 reduce_sum.99
  272.4 4.3 %fusion.7 = f32[384,1536]{1,0:T(8,128)} fusion(f32[384,1536]{1,0:T(8,128)} %get-tuple-element.3, f32[384,1536]{1,0:T(8,128)S(1)} %get-tuple-element.7, f32[1536]{0:T(1024)S(1)} %reduce_sum.99, f32[1536]{0:T(1024)S(1)} %reduce_sum.95, f32[384]{0:T(512)S(1)} %maximum_select_fusion.1, f32[384]{0:T(512)S(1)} %reduce_max.91, s32[1536]{0:T(1024)S(1)} %iota_add_fusion, ...), kind=kLoop, calls=%fused_computation.17 | loop fusion | flops 10616832 | bytes 7100928 | tf_op jit(solution)/shard_map/add | solution.py:80
  (25 shorter events, 0.3 us)
Async XLA Ops:
  7.2 117.1 %copy-start.1 = (f32[384]{0:T(512)S(1)}, f32[384]{0:T(512)}, u32[]{:S(2)}) copy-start(f32[384]{0:T(512)} %param.3) | copy-start | bytes 4612
  7.2 116.0 %all-reduce.2.cloned.1.call-start = ((), (), s32[]{:S(2)}) async-start(), calls=%async_computation | async-start | bytes 393216 | tf_op jit(solution)/shard_map/psum | solution.py:13
  199.1 1.4 copy-start
Sparse Core Ops, SparseCore 0:
  60.3 62.7 all-reduce.1

commit v2 on v0

--- a/solution.py
+++ b/solution.py
@@ -5,6 +5,13 @@
 
 ITERS = 2
 DAMPING = 0.5
+
+
+def solve_slabs_now(x_part):
+    step_out = lax.psum(1, "col")
+    wide_out = jnp.stack(step_out * [x_part], axis=0)
+    near = lax.all_to_all(wide_out, "col", 0, 0)
+    return jnp.concatenate(near, axis=0)
 
 
 def broadcast(block, axis, source):
@@ -59,7 +66,7 @@
         summed = avail + sim
         local_first, local_second = top_two(summed)
         firsts, seconds = (
-            lax.all_gather(local_first, "col", axis=0, tiled=True),
+            solve_slabs_now(local_first),
             lax.all_gather(local_second, "col", axis=0, tiled=True),
         )
         firsts = firsts.reshape(cols_n, row_count)

time: 338 us -> 325 us (0.962)
  blocking collectives: 244 us -> 224 us
  starting transfers between devices: 0.04 us -> 6.71 us
    all_gather x2 -> x0, blocking collectives: 22.4 us -> none  [local(): lax.all_gather(local_first, 'col', axis=0, tiled=True)]
    all_to_all x0 -> x2, starting transfers between devices: none -> 6.68 us  [solve_slabs_now(): near = lax.all_to_all(wide_out, 'col', 0, 0)]
  transfers between devices with their start and end apart: 1 -> 3, of which waited for: 1 -> 1; matrix products, arithmetic and copies ran while one was open for 0% -> 0% of each run, Pallas kernels for 0% -> 0%
where the time goes in v2:
time: 325 us
  blocking collectives  224 us (69%)
  waiting for transfers between devices  62.6 us (19%)
  between operations  14.2 us (4%)
  other arithmetic  13.7 us (4%)
  starting transfers between devices  6.71 us (2%)
    psum x2, blocking collectives, local(): colsum = lax.psum(jnp.sum(positive, axis=0), 'row')  147 us
    psum x1, waiting for transfers between devices, broadcast(): return lax.psum(block, axis)  62.6 us
    all_gather x1, blocking collectives, local(): lax.all_gather(embedding, 'row', axis=1, tiled=True)  52.2 us
    all_gather x2, blocking collectives, local(): lax.all_gather(local_second, 'col', axis=0, tiled=True)  24.5 us
    all_to_all x2, starting transfers between devices, solve_slabs_now(): near = lax.all_to_all(wide_out, 'col', 0, 0)  6.68 us
  transfers between devices with their start and end apart: 3, of which 1 were waited for; matrix products, arithmetic and copies ran while one was open for 0% of the time, Pallas kernels for 0%

profile of v2, /device:TPU:32, one launch (start us, length us, event | category | flops | bytes accessed | tf_op | source)
XLA Modules:
  0.0 324.8 jit_solution(3926164239263136791)
XLA Ops:
  7.2 52.2 %all_gather.9 = bf16[1,32,48,256]{3,2,0,1:T(8,128)(2,1)S(1)} all-gather(bf16[1,1,48,256]{3,2,0,1:T(8,128)(2,1)} %bitcast.12), channel_id=1, replica_groups=mesh['row'=32,'col'=8] {'row'}, dimensions={1}, use_global_device_ids=true | all-gather | bytes 811008 | tf_op jit(solution)/shard_map/all_gather | solution.py:55
  59.5 0.7 dynamic-slice_select_fusion
  60.2 0.3 multiply_reduce_fusion
  60.5 0.1 sub.47
  60.6 62.6 %all-reduce.2.cloned.1.call-done = bf16[384,256]{1,0:T(8,128)(2,1)} async-done(((bf16[384,256]{1,0:T(8,128)(2,1)}), bf16[384,256]{1,0:T(8,128)(2,1)}) %all-reduce.2.cloned.1.call-update) | async-done | bytes 196624 | tf_op jit(solution)/shard_map/psum | solution.py:19
  123.2 1.1 multiply_reduce_fusion.1
  124.2 1.7 fusion.15
  126.0 0.4 fusion.3
  126.4 0.4 fusion.2
  126.8 0.6 stack.4
  127.4 3.3 %all-to-all-start = ((f32[8,1,384]{2,1,0:T(1,128)}), f32[8,1,384]{2,1,0:T(1,128)S(1)}, u32[]{:S(2)}, u32[]{:S(2)}) async-start(f32[8,1,384]{2,1,0:T(1,128)} %stack.4), calls=%async_computation | async-start | bytes 24576 | tf_op jit(solution)/shard_map/all_to_all | solution.py:13
  130.8 12.2 %all-gather = f32[8,1,384]{2,1,0:T(1,128)S(1)} all-gather(f32[1,1,384]{2,1,0:T(1,128)S(1)} %reshape.73), channel_id=1, replica_groups=mesh['row'=32,'col'=8] {'col'}, dimensions={0}, use_global_device_ids=true | all-gather | bytes 13824 | tf_op jit(solution)/shard_map/all_gather | solution.py:70
  143.1 0.7 fusion.9
  143.9 72.6 %psum.22 = f32[1536]{0:T(1024)S(1)} all-reduce(f32[1536]{0:T(1024)S(1)} %fusion.9), channel_id=1, replica_groups=mesh['row'=32,'col'=8] {'row'}, use_global_device_ids=true, to_apply=%region_11.12 | all-reduce | flops 1536 | bytes 12288 | tf_op jit(solution)/shard_map/psum | solution.py:82
  216.5 1.3 fusion.14
  217.8 0.4 fusion.4
  218.2 0.4 fusion.5
  218.6 0.6 copy-done
  219.2 0.6 stack.5
  219.8 3.3 %all-to-all-start.1 = ((f32[8,1,384]{2,1,0:T(1,128)}), f32[8,1,384]{2,1,0:T(1,128)S(1)}, u32[]{:S(2)}, u32[]{:S(2)}) async-start(f32[8,1,384]{2,1,0:T(1,128)} %stack.5), calls=%async_computation.1 | async-start | bytes 24576 | tf_op jit(solution)/shard_map/all_to_all | solution.py:13
  223.1 12.3 %all-gather.1 = f32[8,1,384]{2,1,0:T(1,128)S(1)} all-gather(f32[1,1,384]{2,1,0:T(1,128)S(1)} %reshape.75), channel_id=1, replica_groups=mesh['row'=32,'col'=8] {'col'}, dimensions={0}, use_global_device_ids=true | all-gather | bytes 13824 | tf_op jit(solution)/shard_map/all_gather | solution.py:70
  235.6 3.5 %fusion.8 = (f32[1536]{0:T(1024)S(1)}, f32[384,1536]{1,0:T(8,128)}) fusion(s32[1536]{0:T(1024)S(1)} %iota_add_fusion, s32[384]{0:T(512)S(1)} %iota_add_fusion.1, f32[384,1536]{1,0:T(8,128)S(1)} %get-tuple-element.7, f32[384]{0:T(512)S(1)} %maximum_select_fusion, f32[384,1536]{1,0:T(8,128)} %copy-done, f32[384]{0:T(512)S(1)} %reduce_max.96, ...), kind=kLoop, calls=%fused_computation.21 | loop fusion | flops 7666176 | bytes 7097856 | tf_op jit(solution)/shard_map/reduce_sum | solution.py:82
  239.1 74.6 %psum.23 = f32[1536]{0:T(1024)S(1)} all-reduce(f32[1536]{0:T(1024)S(1)} %get-tuple-element.2), channel_id=1, replica_groups=mesh['row'=32,'col'=8] {'row'}, use_global_device_ids=true, to_apply=%region_20.21 | all-reduce | flops 1536 | bytes 12288 | tf_op jit(solution)/shard_map/psum | solution.py:82
  313.7 4.3 %fusion.7 = f32[384,1536]{1,0:T(8,128)} fusion(f32[384,1536]{1,0:T(8,128)} %get-tuple-element.3, f32[384,1536]{1,0:T(8,128)S(1)} %get-tuple-element.7, f32[1536]{0:T(1024)S(1)} %psum.23, f32[1536]{0:T(1024)S(1)} %psum.22, f32[384]{0:T(512)S(1)} %maximum_select_fusion.1, f32[384]{0:T(512)S(1)} %reduce_max.91, s32[1536]{0:T(1024)S(1)} %iota_add_fusion, ...), kind=kLoop, calls=%fused_computation.17 | loop fusion | flops 10616832 | bytes 7100928 | tf_op jit(solution)/shard_map/add | solution.py:85
  (23 shorter events, 0.3 us)
Async XLA Ops:
  7.2 117.1 %copy-start.1 = (f32[384]{0:T(512)S(1)}, f32[384]{0:T(512)}, u32[]{:S(2)}) copy-start(f32[384]{0:T(512)} %param.3) | copy-start | bytes 4612
  7.2 116.0 %all-reduce.2.cloned.1.call-start = ((), (), s32[]{:S(2)}) async-start(), calls=%async_computation.2 | async-start | bytes 393216 | tf_op jit(solution)/shard_map/psum | solution.py:19
  127.4 15.6 %all-to-all-start = ((f32[8,1,384]{2,1,0:T(1,128)}), f32[8,1,384]{2,1,0:T(1,128)S(1)}, u32[]{:S(2)}, u32[]{:S(2)}) async-start(f32[8,1,384]{2,1,0:T(1,128)} %stack.4), calls=%async_computation | async-start | bytes 24576 | tf_op jit(solution)/shard_map/all_to_all | solution.py:13
  217.7 1.4 copy-start
  219.8 15.7 %all-to-all-start.1 = ((f32[8,1,384]{2,1,0:T(1,128)}), f32[8,1,384]{2,1,0:T(1,128)S(1)}, u32[]{:S(2)}, u32[]{:S(2)}) async-start(f32[8,1,384]{2,1,0:T(1,128)} %stack.5), calls=%async_computation.1 | async-start | bytes 24576 | tf_op jit(solution)/shard_map/all_to_all | solution.py:13
Sparse Core Ops, SparseCore 0:
  60.3 62.7 all-reduce.1
